TPU v7x, 512 devices: a whole 4x4x16 slice. The times are simulated.
512 devices in a mesh: occ: 16 (over y, z_hi), vir: 32 (over x, z_lo, core).
Axes of the slice: x: 4, y: 4, z: 16 (z_hi: 4, z_lo: 4; z = z_hi * 4 + z_lo), core: 2. Of those that a mesh axis runs over, the one named last changes fastest.
Arguments:
- amplitudes: float32 [4, 1024, 1024], P(None, 'occ', 'vir'), may hold values from -6 to 6
- integrals: float32 [4, 28672, 1024], P(None, 'vir', 'occ'), may hold values from -0.1875 to 0.1875
Outputs:
- ladder: float32 [4, 1024, 28672], P(None, 'occ', 'vir')
All inputs are finite; a program needn't handle non-finite values.
Results may differ from a plain program's by a relative error of at most 0.000073.
Values sent between devices are 32-bit elements; how exact they have to be, the bound alone decides.
A program may use at most 64 MiB of HBM per device.

v0:
```python
import jax
import jax.numpy as jnp
from jax import lax
from jax.sharding import PartitionSpec as P


def contract_block(left, piece):
    return lax.dot_general(
        left,
        piece,
        (((2,), (2,)), ((0,), (0,))),
        precision=lax.Precision.HIGHEST,
        preferred_element_type=jnp.float32,
    )


def body(amplitudes, integrals):
    gathered = lax.all_gather(amplitudes, "vir", axis=2, tiled=True)
    panel_sum = contract_block(gathered, lax.all_gather(integrals, "occ", axis=2, tiled=True))
    return 0.5 * panel_sum


def solution(mesh):
    in_specs = (P(None, "occ", "vir"), P(None, "vir", "occ"))
    out_specs = P(None, "occ", "vir")
    return jax.shard_map(body, mesh=mesh, in_specs=in_specs, out_specs=out_specs, check_vma=False)
```

profile of v0, /device:TPU:9, one launch (start us, length us, event | category | flops | bytes accessed | tf_op | source)
XLA Modules:
  0.0 446.1 jit_solution(8332519620568645044)
XLA Ops:
  6.5 0.0 all-gather.3.cloned.1.call-start
  6.5 0.7 all-gather.3.cloned.1.call-update
  7.3 0.0 all-gather.5.cloned.1.call-start
  7.3 0.7 all-gather.5.cloned.1.call-update
  8.0 71.1 %all-gather.3.cloned.1.call-done = f32[4,64,1024]{1,2,0:T(8,128)} async-done(((f32[4,64,32]{1,2,0:T(8,128)}), f32[4,64,1024]{1,2,0:T(8,128)}) %all-gather.3.cloned.1.call-update) | async-done | bytes 1048592 | tf_op jit(solution)/shard_map/all_gather | solution.py:18
  79.1 347.4 %all-gather.5.cloned.1.call-done = f32[4,896,1024]{1,2,0:T(8,128)} async-done(((f32[4,896,64]{1,2,0:T(8,128)}), f32[4,896,1024]{1,2,0:T(8,128)}) %all-gather.5.cloned.1.call-update) | async-done | bytes 14680080 | tf_op jit(solution)/shard_map/all_gather | solution.py:19
  426.6 12.7 %convolution_multiply_fusion = f32[4,64,896]{2,1,0:T(8,128)} fusion(f32[4,64,1024]{1,2,0:T(8,128)} %all-gather.3.cloned.1.call-done, f32[4,896,1024]{1,2,0:T(8,128)} %all-gather.5.cloned.1.call-done), kind=kOutput, calls=%fused_computation | convolution fusion | flops 2818801664 | bytes 16646144 | tf_op jit(solution)/shard_map/dot_general | solution.py:8
Async XLA Ops:
  6.5 72.6 %all-gather.3.cloned.1.call-start = ((), (), s32[]{:S(2)}) async-start(), calls=%async_computation | async-start | bytes 2162688 | tf_op jit(solution)/shard_map/all_gather | solution.py:18
  7.3 419.3 %all-gather.5.cloned.1.call-start = ((), (), s32[]{:S(2)}) async-start(), calls=%async_computation.1 | async-start | bytes 15597568 | tf_op jit(solution)/shard_map/all_gather | solution.py:19
Sparse Core Ops, SparseCore 0:
  9.5 69.5 all-gather.2
  82.1 344.3 all-gather.4
where the time goes:
time: 446 us
  waiting for transfers between devices  420 us (94%)
  between operations  13.4 us (3%)
  matrix products  12.7 us (3%)
    all_gather x1, waiting for transfers between devices, body(): lax.all_gather(integrals, 'occ', axis=2, tiled=True)  347 us
    all_gather x1, waiting for transfers between devices, body(): gathered = lax.all_gather(amplitudes, 'vir', axis=2, tiled=True)  71.1 us
    dot_general x1, matrix products, contract_block(): lax.dot_general(left, piece, (((2,), (2,)), ((0,), (0,))), precision=lax....  12.7 us
  transfers between devices with their start and end apart: 2, of which 2 were waited for; matrix products, arithmetic and copies ran while one was open for 0% of the time, Pallas kernels for 0%

commit v1 on v0

--- a/solution.py
+++ b/solution.py
@@ -15,7 +15,15 @@
 
 
 def body(amplitudes, integrals):
-    gathered = lax.all_gather(amplitudes, "vir", axis=2, tiled=True)
+    gathered = jnp.concatenate(
+        jax.lax.all_to_all(
+            jnp.stack([amplitudes] * jax.lax.axis_size("vir"), axis=0),
+            "vir",
+            split_axis=0,
+            concat_axis=0,
+        ),
+        2,
+    )
     panel_sum = contract_block(gathered, lax.all_gather(integrals, "occ", axis=2, tiled=True))
     return 0.5 * panel_sum
 

time: 446 us -> 387 us (0.87)
  waiting for transfers between devices: 420 us -> 277 us
  blocking collectives: 0 us -> 77.4 us
    all_to_all x0 -> x1, blocking collectives: none -> 77.4 us  [body(): jax.lax.all_to_all(jnp.stack([amplitudes] * jax.lax.axis_size('vir'), axi...]
    all_gather x1, waiting for transfers between devices: 347 us -> 276 us  [body(): lax.all_gather(integrals, 'occ', axis=2, tiled=True)]
    all_gather x1 -> x0, waiting for transfers between devices: 71.1 us -> none  [body(): gathered = lax.all_gather(amplitudes, 'vir', axis=2, tiled=True)]
  transfers between devices with their start and end apart: 2 -> 1, of which waited for: 2 -> 1; matrix products, arithmetic and copies ran while one was open for 0% -> 2% of each run, Pallas kernels for 0% -> 0%
where the time goes in v1:
time: 387 us
  waiting for transfers between devices  277 us (72%)
  blocking collectives  77.4 us (20%)
  between operations  13.4 us (3%)
  matrix products  12.4 us (3%)
    all_gather x1, waiting for transfers between devices, body(): lax.all_gather(integrals, 'occ', axis=2, tiled=True)  276 us
    all_to_all x1, blocking collectives, body(): jax.lax.all_to_all(jnp.stack([amplitudes] * jax.lax.axis_size('vir'), axi...  77.4 us
    dot_general x1, matrix products, contract_block(): lax.dot_general(left, piece, (((2,), (2,)), ((0,), (0,))), precision=lax....  12.4 us
  transfers between devices with their start and end apart: 1, of which 1 were waited for; matrix products, arithmetic and copies ran while one was open for 2% of the time, Pallas kernels for 0%

profile of v1, /device:TPU:9, one launch (start us, length us, event | category | flops | bytes accessed | tf_op | source)
XLA Modules:
  0.0 386.5 jit_solution(5843839390117461624)
XLA Ops:
  6.5 0.0 copy-start
  6.5 0.0 all-gather.2.cloned.1.call-start
  6.5 0.7 all-gather.2.cloned.1.call-update
  7.3 0.1 copy-done
  7.4 0.2 broadcast_bitcast_fusion
  7.6 1.3 reshape.10
  8.9 77.4 %all_to_all.5 = f32[32,1,8192]{2,1,0:T(1,128)S(1)} all-to-all(f32[32,1,8192]{2,1,0:T(1,128)S(1)} %reshape.10), channel_id=1, replica_groups=mesh['occ'=16,'vir'=32] {'vir'}, dimensions={0} | all-to-all | bytes 2097152 | tf_op jit(solution)/shard_map/all_to_all | solution.py:19
  86.4 0.5 broadcast.2
  86.9 3.2 reduce
  90.1 0.8 reshape.11
  90.9 0.2 bitcast_bitcast_fusion
  91.2 0.2 copy.5
  91.4 276.0 %all-gather.2.cloned.1.call-done = f32[4,896,1024]{1,2,0:T(8,128)} async-done(((f32[4,896,64]{1,2,0:T(8,128)}), f32[4,896,1024]{1,2,0:T(8,128)}) %all-gather.2.cloned.1.call-update) | async-done | bytes 14680080 | tf_op jit(solution)/shard_map/all_gather | solution.py:27
  367.3 12.4 %convolution_multiply_fusion = f32[4,64,896]{2,1,0:T(8,128)} fusion(f32[4,64,1024]{1,2,0:T(8,128)S(1)} %bitcast.9, f32[4,896,1024]{1,2,0:T(8,128)} %all-gather.2.cloned.1.call-done), kind=kOutput, calls=%fused_computation | convolution fusion | flops 2818801664 | bytes 16646144 | tf_op jit(solution)/shard_map/dot_general | solution.py:8
Async XLA Ops:
  6.5 0.8 copy-start
  6.5 360.8 %all-gather.2.cloned.1.call-start = ((), (), s32[]{:S(2)}) async-start(), calls=%async_computation.1 | async-start | bytes 15597568 | tf_op jit(solution)/shard_map/all_gather | solution.py:27
Sparse Core Ops, SparseCore 0:
  10.3 356.9 all-gather.1
